TPU v7x, 128 devices: a whole 4x4x4 slice. The times are simulated.
128 devices in a mesh: lat: 8 (over z_hi, x), lon: 16 (over y, z_lo, core).
Axes of the slice: x: 4, y: 4, z: 4 (z_hi: 2, z_lo: 2; z = z_hi * 2 + z_lo), core: 2. Of those that a mesh axis runs over, the one named last changes fastest.
Arguments:
- features: bfloat16 [128, 3072, 128], P('lat', 'lon'), may hold values from -6 to 6
- cotangent: bfloat16 [128, 3072, 128], P('lat', 'lon'), may hold values from -6 to 6
- w_first: bfloat16 [1152, 128], P(('lat', 'lon')), may hold values from -0.1875 to 0.1875
- w_second: bfloat16 [1152, 128], P(('lat', 'lon')), may hold values from -0.1875 to 0.1875
Outputs:
- grad_features: bfloat16 [128, 3072, 128], P('lat', 'lon')
- grad_first: float32 [1152, 128], P(('lat', 'lon'))
- grad_second: float32 [1152, 128], P(('lat', 'lon'))
All inputs are finite; a program needn't handle non-finite values.
Results may differ from a plain program's by a relative error of at most 0.0033.
Values may be sent and summed in bfloat16 or wider, within the bound.
No kernel may reach another device: no remote copies, remote signals or barrier semaphores. Data moves between devices by JAX's collectives and lax.ppermute only.
A program may use at most 64 MiB of HBM per device.

v0:
```python
import jax
import jax.numpy as jnp
from jax import lax
from jax.sharding import PartitionSpec as P


def padded_2(block, sides, width, periodic):
    for axis, dim in sides:
        count = lax.axis_size(axis)
        forward = [(i, i + 1) for i in range(count - 1)]
        if periodic:
            forward.append((count - 1, 0))
        backward = [(target, source) for source, target in forward]
        low = lax.ppermute(
            lax.slice_in_dim(block, block.shape[dim] - width, None, axis=dim), axis, forward
        )
        high = lax.ppermute(lax.slice_in_dim(block, 0, width, axis=dim), axis, backward)
        block = jnp.concatenate([low, block, high], axis=dim)
    return block


def add_rims(field, width):
    field = padded_2(field, (("lon", 1),), width, True)
    return padded_2(field, (("lat", 0),), width, False)


def forward_conv(padded, weight, rows, cols):
    chans = padded.shape[2]
    total = jnp.zeros((rows * cols, weight.shape[1]), jnp.float32)
    for tap in range(9):
        shift_r, shift_c = divmod(tap, 3)
        piece = padded[shift_r : shift_r + rows, shift_c : shift_c + cols].reshape(-1, chans)
        total = total + jnp.dot(
            piece, weight[tap * chans : (tap + 1) * chans], preferred_element_type=jnp.float32
        )
    return total.reshape(rows, cols, -1)


def transpose_conv(padded, weight, rows, cols):
    chans = weight.shape[1]
    inner = weight.shape[0] // 9
    total = jnp.zeros((rows * cols, inner), jnp.float32)
    for tap in range(9):
        shift_r, shift_c = divmod(tap, 3)
        piece = padded[2 - shift_r : 2 - shift_r + rows, 2 - shift_c : 2 - shift_c + cols].reshape(
            -1, chans
        )
        block = weight[tap * inner : (tap + 1) * inner]
        total = total + lax.dot_general(
            piece, block, (((1,), (1,)), ((), ())), preferred_element_type=jnp.float32
        )
    return total.reshape(rows, cols, -1)


def weight_grad(padded, grad_out, rows, cols):
    chans = padded.shape[2]
    flat_grad = grad_out.reshape(-1, grad_out.shape[2])
    blocks = []
    for tap in range(9):
        shift_r, shift_c = divmod(tap, 3)
        piece = padded[shift_r : shift_r + rows, shift_c : shift_c + cols].reshape(-1, chans)
        blocks.append(
            lax.dot_general(
                piece, flat_grad, (((0,), (0,)), ((), ())), preferred_element_type=jnp.float32
            )
        )
    return jnp.concatenate(blocks, 0)


def local(features, cotangent, w_first, w_second):
    rows, cols, chans = (features.shape[0], features.shape[1], features.shape[2])
    kernel_one, kernel_two = (
        lax.all_gather(w_first, ("lat", "lon"), axis=0, tiled=True),
        lax.all_gather(w_second, ("lat", "lon"), axis=0, tiled=True),
    )
    feat_pad = add_rims(features, 1)
    grad_pad = add_rims(cotangent, 1)
    pre = forward_conv(feat_pad, kernel_one, rows, cols)
    act_pad = add_rims(jax.nn.silu(pre).astype(jnp.bfloat16), 1)
    second_terms = weight_grad(act_pad, cotangent, rows, cols)
    back_act = transpose_conv(grad_pad, kernel_two, rows, cols)
    sigma = jax.nn.sigmoid(pre)
    back_pre = (back_act * sigma * (1.0 + pre * (1.0 - sigma))).astype(jnp.bfloat16)
    first_terms = weight_grad(feat_pad, back_pre, rows, cols)
    back_pad = add_rims(back_pre, 1)
    grad_features = (
        cotangent.astype(jnp.float32) + transpose_conv(back_pad, kernel_one, rows, cols)
    ).astype(jnp.bfloat16)
    grad_first, grad_second = (
        lax.psum_scatter(first_terms, ("lat", "lon"), scatter_dimension=0, tiled=True),
        lax.psum_scatter(second_terms, ("lat", "lon"), scatter_dimension=0, tiled=True),
    )
    return (grad_features, grad_first, grad_second)


def solution(mesh):
    in_specs = (
        P("lat", "lon", None),
        P("lat", "lon", None),
        P(("lat", "lon"), None),
        P(("lat", "lon"), None),
    )
    out_specs = (P("lat", "lon", None), P(("lat", "lon"), None), P(("lat", "lon"), None))
    return jax.shard_map(local, mesh=mesh, in_specs=in_specs, out_specs=out_specs, check_vma=False)
```

profile of v0, /device:TPU:1, one launch (start us, length us, event | category | flops | bytes accessed | tf_op | source)
XLA Modules:
  0.0 589.7 jit_solution(9573633949376731134)
XLA Ops:
  8.1 3.1 collective-permute-start
  12.0 1.8 collective-permute-start.4
  14.5 179.7 %all-gather = bf16[128,9,128]{2,1,0:T(8,128)(2,1)S(1)} all-gather(bf16[1,9,128]{2,1,0:T(8,128)(2,1)} %bitcast.182), channel_id=1, replica_groups=mesh['lat'=8,'lon'=16] {'lat','lon'}, dimensions={0}, use_global_device_ids=true | all-gather | bytes 297216 | tf_op jit(solution)/shard_map/all_gather | solution.py:74
  194.3 172.1 %all-gather.1 = bf16[128,9,128]{2,1,0:T(8,128)(2,1)S(1)} all-gather(bf16[1,9,128]{2,1,0:T(8,128)(2,1)} %bitcast.183), channel_id=1, replica_groups=mesh['lat'=8,'lon'=16] {'lat','lon'}, dimensions={0}, use_global_device_ids=true | all-gather | bytes 297216 | tf_op jit(solution)/shard_map/all_gather | solution.py:73
  366.6 1.5 fusion.38
  368.2 1.5 fusion.56
  369.7 1.3 collective-permute-start.2
  371.0 4.0 collective-permute-start.3
  375.1 1.9 collective-permute-start.6
  377.0 1.5 collective-permute-start.7
  382.2 1.1 fusion.81
  390.6 1.9 fusion.32
  393.3 3.2 collective-permute-start.12
  400.3 1.8 collective-permute-start.8
  403.1 2.8 collective-permute-start.14
  405.9 1.3 collective-permute-start.15
  407.3 1.3 collective-permute-start.10
  408.6 4.6 collective-permute-start.11
  413.2 1.6 pad_maximum_fusion.8
  415.2 1.0 fusion.14
  418.4 1.1 fusion.11
  419.4 1.0 fusion.10
  420.5 1.0 fusion.9
  422.6 1.0 fusion.7
  425.1 1.6 fusion.78
  426.6 1.5 fusion.62
  428.2 1.4 fusion.77
  429.9 2.1 convolution_add_fusion.5
  436.7 1.1 add_convert_fusion
  437.8 142.4 %all-reduce.5.cloned.1.call-done = (f32[1152,128]{1,0:T(8,128)}, f32[1152,128]{1,0:T(8,128)}) async-done(((f32[1152,128]{1,0:T(8,128)}, f32[1152,128]{1,0:T(8,128)}), (f32[1152,128]{1,0:T(8,128)}, f32[1152,128]{1,0:T(8,128)})) %all-reduce.5.cloned.1.call-update) | async-done | bytes 1179664
  580.2 1.3 constant_dynamic-slice_fusion
  581.5 1.3 constant_dynamic-slice_fusion.1
  (95 shorter events, 29.2 us)
Async XLA Ops:
  7.2 359.5 %copy-start = (bf16[16,192,128]{2,1,0:T(8,128)(2,1)S(1)}, bf16[16,192,128]{2,1,0:T(8,128)(2,1)}, u32[]{:S(2)}) copy-start(bf16[16,192,128]{2,1,0:T(8,128)(2,1)} %param.5) | copy-start | bytes 2359300
  7.2 573.0 %all-reduce.5.cloned.1.call-start = ((), (), s32[]{:S(2)}) async-start(), calls=%async_computation | async-start | bytes 2359296
  8.1 361.6 %collective-permute-start = (bf16[16,1,128]{2,1,0:T(2,128)(2,1)S(1)}, bf16[16,1,128]{2,1,0:T(2,128)(2,1)S(1)}, u32[]{:S(2)}, u32[]{:S(2)}) collective-permute-start(bf16[16,1,128]{2,1,0:T(2,128)(2,1)S(1)} %get-tuple-element.49), channel_id=1, source_target_pairs={{0,1},{1,2},{2,3},{3,4},{4,5},{5,6},{6,7},{7,8},{8,9},{9,10},{10,1... | collective-permute-start | bytes 12296 | tf_op jit(solution)/shard_map/ppermute | solution.py:14
  11.2 358.5 %collective-permute-start.1 = (bf16[16,1,128]{2,1,0:T(2,128)(2,1)S(1)}, bf16[16,1,128]{2,1,0:T(2,128)(2,1)S(1)}, u32[]{:S(2)}, u32[]{:S(2)}) collective-permute-start(bf16[16,1,128]{2,1,0:T(2,128)(2,1)S(1)} %get-tuple-element.50), channel_id=1, source_target_pairs={{1,0},{2,1},{3,2},{4,3},{5,4},{6,5},{7,6},{8,7},{9,8},{10,9},{11,1... | collective-permute-start | bytes 12296 | tf_op jit(solution)/shard_map/ppermute | solution.py:17
  12.0 363.1 %collective-permute-start.4 = (bf16[16,1,128]{2,1,0:T(2,128)(2,1)S(1)}, bf16[16,1,128]{2,1,0:T(2,128)(2,1)S(1)}, u32[]{:S(2)}, u32[]{:S(2)}) collective-permute-start(bf16[16,1,128]{2,1,0:T(2,128)(2,1)S(1)} %get-tuple-element.53), channel_id=1, source_target_pairs={{0,1},{1,2},{2,3},{3,4},{4,5},{5,6},{6,7},{7,8},{8,9},{9,10},{10,1... | collective-permute-start | bytes 12296 | tf_op jit(solution)/shard_map/ppermute | solution.py:14
  13.8 361.3 %collective-permute-start.5 = (bf16[16,1,128]{2,1,0:T(2,128)(2,1)S(1)}, bf16[16,1,128]{2,1,0:T(2,128)(2,1)S(1)}, u32[]{:S(2)}, u32[]{:S(2)}) collective-permute-start(bf16[16,1,128]{2,1,0:T(2,128)(2,1)S(1)} %get-tuple-element.54), channel_id=1, source_target_pairs={{1,0},{2,1},{3,2},{4,3},{5,4},{6,5},{7,6},{8,7},{9,8},{10,9},{11,1... | collective-permute-start | bytes 12296 | tf_op jit(solution)/shard_map/ppermute | solution.py:17
  366.5 1.7 copy-start.1
  369.7 9.7 %collective-permute-start.2 = (bf16[1,194,128]{2,1,0:T(8,128)(2,1)S(1)}, bf16[1,194,128]{2,1,0:T(8,128)(2,1)S(1)}, u32[]{:S(2)}, u32[]{:S(2)}) collective-permute-start(bf16[1,194,128]{2,1,0:T(8,128)(2,1)S(1)} %get-tuple-element.35), channel_id=1, source_target_pairs={{16,0},{32,16},{48,32},{64,48},{80,64},{96,80},{112,96},{17,1},{33... | collective-permute-start | bytes 149000 | tf_op jit(solution)/shard_map/ppermute | solution.py:17
  371.0 8.4 %collective-permute-start.3 = (bf16[1,194,128]{2,1,0:T(8,128)(2,1)S(1)}, bf16[1,194,128]{2,1,0:T(8,128)(2,1)S(1)}, u32[]{:S(2)}, u32[]{:S(2)}) collective-permute-start(bf16[1,194,128]{2,1,0:T(8,128)(2,1)S(1)} %get-tuple-element.36), channel_id=1, source_target_pairs={{0,16},{16,32},{32,48},{48,64},{64,80},{80,96},{96,112},{1,17},{17... | collective-permute-start | bytes 149000 | tf_op jit(solution)/shard_map/ppermute | solution.py:14
  375.1 6.4 %collective-permute-start.6 = (bf16[1,194,128]{2,1,0:T(8,128)(2,1)S(1)}, bf16[1,194,128]{2,1,0:T(8,128)(2,1)S(1)}, u32[]{:S(2)}, u32[]{:S(2)}) collective-permute-start(bf16[1,194,128]{2,1,0:T(8,128)(2,1)S(1)} %get-tuple-element.39), channel_id=1, source_target_pairs={{0,16},{16,32},{32,48},{48,64},{64,80},{80,96},{96,112},{1,17},{17... | collective-permute-start | bytes 149000 | tf_op jit(solution)/shard_map/ppermute | solution.py:14
  377.0 4.9 collective-permute-start.7
  384.4 1.4 copy-start.3
  387.7 1.4 copy-start.2
  393.3 9.8 %collective-permute-start.12 = (bf16[16,1,128]{2,1,0:T(2,128)(2,1)S(1)}, bf16[16,1,128]{2,1,0:T(2,128)(2,1)S(1)}, u32[]{:S(2)}, u32[]{:S(2)}) collective-permute-start(bf16[16,1,128]{2,1,0:T(2,128)(2,1)S(1)} %get-tuple-element.41), channel_id=1, source_target_pairs={{0,1},{1,2},{2,3},{3,4},{4,5},{5,6},{6,7},{7,8},{8,9},{9,10},{10,1... | collective-permute-start | bytes 12296 | tf_op jit(solution)/shard_map/ppermute | solution.py:14
  396.5 6.6 %collective-permute-start.13 = (bf16[16,1,128]{2,1,0:T(2,128)(2,1)S(1)}, bf16[16,1,128]{2,1,0:T(2,128)(2,1)S(1)}, u32[]{:S(2)}, u32[]{:S(2)}) collective-permute-start(bf16[16,1,128]{2,1,0:T(2,128)(2,1)S(1)} %get-tuple-element.42), channel_id=1, source_target_pairs={{1,0},{2,1},{3,2},{4,3},{5,4},{6,5},{7,6},{8,7},{9,8},{10,9},{11,1... | collective-permute-start | bytes 12296 | tf_op jit(solution)/shard_map/ppermute | solution.py:17
  400.3 14.6 %copy-start.9 = (f32[1152,128]{1,0:T(8,128)}, f32[1152,128]{1,0:T(8,128)S(1)}, u32[]{:S(2)}) copy-start(f32[1152,128]{1,0:T(8,128)S(1)} %fusion.15) | copy-start | bytes 1769476
  400.3 6.9 %collective-permute-start.8 = (bf16[16,1,128]{2,1,0:T(2,128)(2,1)S(1)}, bf16[16,1,128]{2,1,0:T(2,128)(2,1)S(1)}, u32[]{:S(2)}, u32[]{:S(2)}) collective-permute-start(bf16[16,1,128]{2,1,0:T(2,128)(2,1)S(1)} %get-tuple-element.45), channel_id=1, source_target_pairs={{0,1},{1,2},{2,3},{3,4},{4,5},{5,6},{6,7},{7,8},{8,9},{9,10},{10,1... | collective-permute-start | bytes 12296 | tf_op jit(solution)/shard_map/ppermute | solution.py:14
  402.1 5.1 collective-permute-start.9
  403.1 11.7 %collective-permute-start.14 = (bf16[1,194,128]{2,1,0:T(8,128)(2,1)S(1)}, bf16[1,194,128]{2,1,0:T(8,128)(2,1)S(1)}, u32[]{:S(2)}, u32[]{:S(2)}) collective-permute-start(bf16[1,194,128]{2,1,0:T(8,128)(2,1)S(1)} %get-tuple-element.28), channel_id=1, source_target_pairs={{0,16},{16,32},{32,48},{48,64},{64,80},{80,96},{96,112},{1,17},{17... | collective-permute-start | bytes 149000 | tf_op jit(solution)/shard_map/ppermute | solution.py:14
  405.9 8.9 %collective-permute-start.15 = (bf16[1,194,128]{2,1,0:T(8,128)(2,1)S(1)}, bf16[1,194,128]{2,1,0:T(8,128)(2,1)S(1)}, u32[]{:S(2)}, u32[]{:S(2)}) collective-permute-start(bf16[1,194,128]{2,1,0:T(8,128)(2,1)S(1)} %get-tuple-element.27), channel_id=1, source_target_pairs={{16,0},{32,16},{48,32},{64,48},{80,64},{96,80},{112,96},{17,1},{33... | collective-permute-start | bytes 149000 | tf_op jit(solution)/shard_map/ppermute | solution.py:17
  407.3 17.4 %collective-permute-start.10 = (bf16[1,194,128]{2,1,0:T(8,128)(2,1)S(1)}, bf16[1,194,128]{2,1,0:T(8,128)(2,1)S(1)}, u32[]{:S(2)}, u32[]{:S(2)}) collective-permute-start(bf16[1,194,128]{2,1,0:T(8,128)(2,1)S(1)} %get-tuple-element.31), channel_id=1, source_target_pairs={{16,0},{32,16},{48,32},{64,48},{80,64},{96,80},{112,96},{17,1},{33... | collective-permute-start | bytes 149000 | tf_op jit(solution)/shard_map/ppermute | solution.py:17
  408.6 16.1 %collective-permute-start.11 = (bf16[1,194,128]{2,1,0:T(8,128)(2,1)S(1)}, bf16[1,194,128]{2,1,0:T(8,128)(2,1)S(1)}, u32[]{:S(2)}, u32[]{:S(2)}) collective-permute-start(bf16[1,194,128]{2,1,0:T(8,128)(2,1)S(1)} %get-tuple-element.32), channel_id=1, source_target_pairs={{0,16},{16,32},{32,48},{48,64},{64,80},{80,96},{96,112},{1,17},{17... | collective-permute-start | bytes 149000 | tf_op jit(solution)/shard_map/ppermute | solution.py:14
  429.9 2.1 copy-start.5
  432.0 1.1 copy-start.7
  432.0 1.6 copy-start.8
  433.7 1.1 copy-start.6
  434.8 1.1 copy-start.4
Sparse Core Ops, SparseCore 0:
  430.0 150.1 all-reduce.4
where the time goes:
time: 590 us
  blocking collectives  352 us (60%)
  waiting for transfers between devices  143 us (24%)
  starting transfers between devices  30.3 us (5%)
  matrix products  29.7 us (5%)
  between operations  14.5 us (2%)
  local copies, waits for them, and re-layouts  14.4 us (2%)
  other arithmetic  6.05 us (1%)
    all_gather x1, blocking collectives, local(): lax.all_gather(w_second, ('lat', 'lon'), axis=0, tiled=True)  180 us
    all_gather x1, blocking collectives, local(): lax.all_gather(w_first, ('lat', 'lon'), axis=0, tiled=True)  172 us
    unnamed x2, waiting for transfers between devices  142 us
    ppermute x8, starting transfers between devices, padded_2(): lax.ppermute(lax.slice_in_dim(block, block.shape[dim] - width, None, axis...  23.2 us
    dot_general x18, matrix products, weight_grad(): lax.dot_general(piece, flat_grad, (((0,), (0,)), ((), ())), preferred_ele...  13.2 us
    dot_general x18, matrix products, transpose_conv(): lax.dot_general(piece, block, (((1,), (1,)), ((), ())), preferred_element...  12.2 us
  transfers between devices with their start and end apart: 17, of which 2 were waited for; matrix products, arithmetic and copies ran while one was open for 5% of the time, Pallas kernels for 0%

commit v1 on v0

--- a/solution.py
+++ b/solution.py
@@ -70,7 +70,12 @@
 def local(features, cotangent, w_first, w_second):
     rows, cols, chans = (features.shape[0], features.shape[1], features.shape[2])
     kernel_one, kernel_two = (
-        lax.all_gather(w_first, ("lat", "lon"), axis=0, tiled=True),
+        jnp.concatenate(
+            lax.all_to_all(
+                jnp.stack([w_first] * lax.axis_size(("lat", "lon"))), ("lat", "lon"), 0, 0
+            ),
+            axis=0,
+        ),
         lax.all_gather(w_second, ("lat", "lon"), axis=0, tiled=True),
     )
     feat_pad = add_rims(features, 1)

time: 590 us -> 442 us (0.75)
  blocking collectives: 352 us -> 180 us
  starting transfers between devices: 30.3 us -> 42.2 us
  local copies, waits for them, and re-layouts: 14.4 us -> 24.6 us
    all_gather x1 -> x0, blocking collectives: 172 us -> none  [local(): lax.all_gather(w_first, ('lat', 'lon'), axis=0, tiled=True)]
    all_to_all x0 -> x1, starting transfers between devices: none -> 11.6 us  [local(): lax.all_to_all(jnp.stack([w_first] * lax.axis_size(('lat', 'lon'))), ('la...]
    unnamed x24 -> x47, local copies, waits for them, and re-layouts: 7.77 us -> 13.4 us
  transfers between devices with their start and end apart: 17 -> 18, of which waited for: 2 -> 1; matrix products, arithmetic and copies ran while one was open for 5% -> 8% of each run, Pallas kernels for 0% -> 0%
where the time goes in v1:
time: 442 us; the launch traced here: 441 us
  blocking collectives  180 us (41%)
  waiting for transfers between devices  142 us (32%)
  starting transfers between devices  42.2 us (10%)
  matrix products  30.8 us (7%)
  local copies, waits for them, and re-layouts  24.6 us (6%)
  between operations  14.6 us (3%)
  other arithmetic  6.86 us (2%)
    all_gather x1, blocking collectives, local(): lax.all_gather(w_second, ('lat', 'lon'), axis=0, tiled=True)  180 us
    unnamed x2, waiting for transfers between devices  142 us
    ppermute x8, starting transfers between devices, padded_2(): lax.ppermute(lax.slice_in_dim(block, block.shape[dim] - width, None, axis...  20.9 us
    unnamed x47, local copies, waits for them, and re-layouts  13.4 us
    dot_general x18, matrix products, transpose_conv(): lax.dot_general(piece, block, (((1,), (1,)), ((), ())), preferred_element...  13.4 us
    dot_general x18, matrix products, weight_grad(): lax.dot_general(piece, flat_grad, (((0,), (0,)), ((), ())), preferred_ele...  13.1 us
    all_to_all x1, starting transfers between devices, local(): lax.all_to_all(jnp.stack([w_first] * lax.axis_size(('lat', 'lon'))), ('la...  11.6 us
    ppermute x8, starting transfers between devices, padded_2(): lax.ppermute(lax.slice_in_dim(block, 0, width, axis=dim), axis, backward)  9.69 us
  transfers between devices with their start and end apart: 18, of which 1 were waited for; matrix products, arithmetic and copies ran while one was open for 8% of the time, Pallas kernels for 0%

profile of v1, /device:TPU:1, one launch (start us, length us, event | category | flops | bytes accessed | tf_op | source)
XLA Modules:
  0.0 440.5 jit_solution(14837902452169304346)
XLA Ops:
  8.1 3.1 collective-permute-start
  11.9 1.8 collective-permute-start.4
  14.5 1.5 stack.2
  16.0 11.6 %all-to-all-start = ((bf16[128,9,128]{2,1,0:T(8,128)(2,1)}), bf16[128,9,128]{2,1,0:T(8,128)(2,1)}, u32[]{:S(2)}, u32[]{:S(2)}) async-start(bf16[128,9,128]{2,1,0:T(8,128)(2,1)} %stack.2), calls=%async_computation | async-start | bytes 1048576 | tf_op jit(solution)/shard_map/all_to_all | solution.py:74
  27.7 179.7 %all-gather = bf16[128,9,128]{2,1,0:T(8,128)(2,1)S(1)} all-gather(bf16[1,9,128]{2,1,0:T(8,128)(2,1)S(1)} %bitcast.181), channel_id=1, replica_groups=mesh['lat'=8,'lon'=16] {'lat','lon'}, dimensions={0}, use_global_device_ids=true | all-gather | bytes 297216 | tf_op jit(solution)/shard_map/all_gather | solution.py:79
  207.6 1.5 fusion.38
  209.2 1.3 collective-permute-start.2
  210.5 4.0 collective-permute-start.3
  214.5 1.9 collective-permute-start.6
  216.5 1.5 collective-permute-start.7
  218.4 1.3 pad_maximum_fusion.10
  225.1 2.7 fusion.81
  227.8 1.6 convolution_add_fusion.12
  229.3 1.2 reshape.130
  230.5 1.5 fusion.64
  239.9 1.9 fusion.32
  248.7 1.1 collective-permute-start.8
  249.7 2.6 collective-permute-start.9
  252.4 4.3 collective-permute-start.14
  256.7 1.3 collective-permute-start.15
  258.1 1.3 collective-permute-start.10
  259.4 4.6 %collective-permute-start.11 = (bf16[1,194,128]{2,1,0:T(8,128)(2,1)S(1)}, bf16[1,194,128]{2,1,0:T(8,128)(2,1)S(1)}, u32[]{:S(2)}, u32[]{:S(2)}) collective-permute-start(bf16[1,194,128]{2,1,0:T(8,128)(2,1)S(1)} %get-tuple-element.32), channel_id=1, source_target_pairs={{0,16},{16,32},{32,48},{48,64},{64,80},{80,96},{96,112},{1,17},{17... | collective-permute-start | bytes 149000 | tf_op jit(solution)/shard_map/ppermute | solution.py:14
  264.0 1.6 pad_maximum_fusion.8
  271.2 1.1 fusion.9
  275.8 1.6 fusion.78
  277.4 1.5 fusion.62
  278.9 1.5 fusion.77
  280.8 2.1 convolution_add_fusion.5
  288.3 1.1 add_convert_fusion
  289.4 141.7 %all-reduce.5.cloned.1.call-done = (f32[1152,128]{1,0:T(8,128)}, f32[1152,128]{1,0:T(8,128)}) async-done(((f32[1152,128]{1,0:T(8,128)}, f32[1152,128]{1,0:T(8,128)}), (f32[1152,128]{1,0:T(8,128)}, f32[1152,128]{1,0:T(8,128)})) %all-reduce.5.cloned.1.call-update) | async-done | bytes 1179664
  431.0 1.3 constant_dynamic-slice_fusion
  432.4 1.3 constant_dynamic-slice_fusion.1
  (121 shorter events, 37.9 us)
Async XLA Ops:
  7.2 200.4 %copy-start = (bf16[16,192,128]{2,1,0:T(8,128)(2,1)S(1)}, bf16[16,192,128]{2,1,0:T(8,128)(2,1)}, u32[]{:S(2)}) copy-start(bf16[16,192,128]{2,1,0:T(8,128)(2,1)} %param.5) | copy-start | bytes 2359300
  7.2 20.5 %copy-start.21 = (bf16[9,128]{1,0:T(8,128)(2,1)S(1)}, bf16[9,128]{1,0:T(8,128)(2,1)}, u32[]{:S(2)}) copy-start(bf16[9,128]{1,0:T(8,128)(2,1)} %param.7) | copy-start | bytes 6916
  8.1 201.1 %collective-permute-start = (bf16[16,1,128]{2,1,0:T(2,128)(2,1)S(1)}, bf16[16,1,128]{2,1,0:T(2,128)(2,1)S(1)}, u32[]{:S(2)}, u32[]{:S(2)}) collective-permute-start(bf16[16,1,128]{2,1,0:T(2,128)(2,1)S(1)} %get-tuple-element.49), channel_id=1, source_target_pairs={{0,1},{1,2},{2,3},{3,4},{4,5},{5,6},{6,7},{7,8},{8,9},{9,10},{10,1... | collective-permute-start | bytes 12296 | tf_op jit(solution)/shard_map/ppermute | solution.py:14
  11.1 198.0 %collective-permute-start.1 = (bf16[16,1,128]{2,1,0:T(2,128)(2,1)S(1)}, bf16[16,1,128]{2,1,0:T(2,128)(2,1)S(1)}, u32[]{:S(2)}, u32[]{:S(2)}) collective-permute-start(bf16[16,1,128]{2,1,0:T(2,128)(2,1)S(1)} %get-tuple-element.50), channel_id=1, source_target_pairs={{1,0},{2,1},{3,2},{4,3},{5,4},{6,5},{7,6},{8,7},{9,8},{10,9},{11,1... | collective-permute-start | bytes 12296 | tf_op jit(solution)/shard_map/ppermute | solution.py:17
  11.9 202.5 %collective-permute-start.4 = (bf16[16,1,128]{2,1,0:T(2,128)(2,1)S(1)}, bf16[16,1,128]{2,1,0:T(2,128)(2,1)S(1)}, u32[]{:S(2)}, u32[]{:S(2)}) collective-permute-start(bf16[16,1,128]{2,1,0:T(2,128)(2,1)S(1)} %get-tuple-element.53), channel_id=1, source_target_pairs={{0,1},{1,2},{2,3},{3,4},{4,5},{5,6},{6,7},{7,8},{8,9},{9,10},{10,1... | collective-permute-start | bytes 12296 | tf_op jit(solution)/shard_map/ppermute | solution.py:14
  13.7 200.7 %collective-permute-start.5 = (bf16[16,1,128]{2,1,0:T(2,128)(2,1)S(1)}, bf16[16,1,128]{2,1,0:T(2,128)(2,1)S(1)}, u32[]{:S(2)}, u32[]{:S(2)}) collective-permute-start(bf16[16,1,128]{2,1,0:T(2,128)(2,1)S(1)} %get-tuple-element.54), channel_id=1, source_target_pairs={{1,0},{2,1},{3,2},{4,3},{5,4},{6,5},{7,6},{8,7},{9,8},{10,9},{11,1... | collective-permute-start | bytes 12296 | tf_op jit(solution)/shard_map/ppermute | solution.py:17
  16.0 213.3 %all-to-all-start = ((bf16[128,9,128]{2,1,0:T(8,128)(2,1)}), bf16[128,9,128]{2,1,0:T(8,128)(2,1)}, u32[]{:S(2)}, u32[]{:S(2)}) async-start(bf16[128,9,128]{2,1,0:T(8,128)(2,1)} %stack.2), calls=%async_computation | async-start | bytes 1048576 | tf_op jit(solution)/shard_map/all_to_all | solution.py:74
  27.6 403.4 %all-reduce.5.cloned.1.call-start = ((), (), s32[]{:S(2)}) async-start(), calls=%async_computation.1 | async-start | bytes 2359296
  207.6 6.9 %copy-start.1 = (bf16[16,192,128]{2,1,0:T(8,128)(2,1)S(1)}, bf16[16,192,128]{2,1,0:T(8,128)(2,1)}, u32[]{:S(2)}) copy-start(bf16[16,192,128]{2,1,0:T(8,128)(2,1)} %param.4) | copy-start | bytes 2359300
  209.2 10.5 %collective-permute-start.2 = (bf16[1,194,128]{2,1,0:T(8,128)(2,1)S(1)}, bf16[1,194,128]{2,1,0:T(8,128)(2,1)S(1)}, u32[]{:S(2)}, u32[]{:S(2)}) collective-permute-start(bf16[1,194,128]{2,1,0:T(8,128)(2,1)S(1)} %get-tuple-element.35), channel_id=1, source_target_pairs={{16,0},{32,16},{48,32},{64,48},{80,64},{96,80},{112,96},{17,1},{33... | collective-permute-start | bytes 149000 | tf_op jit(solution)/shard_map/ppermute | solution.py:17
  210.5 9.2 %collective-permute-start.3 = (bf16[1,194,128]{2,1,0:T(8,128)(2,1)S(1)}, bf16[1,194,128]{2,1,0:T(8,128)(2,1)S(1)}, u32[]{:S(2)}, u32[]{:S(2)}) collective-permute-start(bf16[1,194,128]{2,1,0:T(8,128)(2,1)S(1)} %get-tuple-element.36), channel_id=1, source_target_pairs={{0,16},{16,32},{32,48},{48,64},{64,80},{80,96},{96,112},{1,17},{17... | collective-permute-start | bytes 149000 | tf_op jit(solution)/shard_map/ppermute | solution.py:14
  214.5 10.1 %collective-permute-start.6 = (bf16[1,194,128]{2,1,0:T(8,128)(2,1)S(1)}, bf16[1,194,128]{2,1,0:T(8,128)(2,1)S(1)}, u32[]{:S(2)}, u32[]{:S(2)}) collective-permute-start(bf16[1,194,128]{2,1,0:T(8,128)(2,1)S(1)} %get-tuple-element.39), channel_id=1, source_target_pairs={{0,16},{16,32},{32,48},{48,64},{64,80},{80,96},{96,112},{1,17},{17... | collective-permute-start | bytes 149000 | tf_op jit(solution)/shard_map/ppermute | solution.py:14
  216.5 8.2 %collective-permute-start.7 = (bf16[1,194,128]{2,1,0:T(8,128)(2,1)S(1)}, bf16[1,194,128]{2,1,0:T(8,128)(2,1)S(1)}, u32[]{:S(2)}, u32[]{:S(2)}) collective-permute-start(bf16[1,194,128]{2,1,0:T(8,128)(2,1)S(1)} %get-tuple-element.40), channel_id=1, source_target_pairs={{16,0},{32,16},{48,32},{64,48},{80,64},{96,80},{112,96},{17,1},{33... | collective-permute-start | bytes 149000 | tf_op jit(solution)/shard_map/ppermute | solution.py:17
  219.7 16.6 %copy-start.4 = (bf16[16,192,128]{2,1,0:T(8,128)(2,1)}, bf16[16,192,128]{2,1,0:T(8,128)(2,1)S(1)}, u32[]{:S(2)}) copy-start(bf16[16,192,128]{2,1,0:T(8,128)(2,1)S(1)} %get-tuple-element.51) | copy-start | bytes 2359300
  222.1 1.4 copy-start.7
  225.1 2.7 copy-start.2
  232.0 1.1 copy-start.9
  232.4 1.2 copy-start.16
  236.3 1.1 copy-start.12
  238.5 1.4 copy-start.8
  241.8 1.9 copy-start.3
  242.6 9.7 %collective-permute-start.12 = (bf16[16,1,128]{2,1,0:T(2,128)(2,1)S(1)}, bf16[16,1,128]{2,1,0:T(2,128)(2,1)S(1)}, u32[]{:S(2)}, u32[]{:S(2)}) collective-permute-start(bf16[16,1,128]{2,1,0:T(2,128)(2,1)S(1)} %get-tuple-element.41), channel_id=1, source_target_pairs={{0,1},{1,2},{2,3},{3,4},{4,5},{5,6},{6,7},{7,8},{8,9},{9,10},{10,1... | collective-permute-start | bytes 12296 | tf_op jit(solution)/shard_map/ppermute | solution.py:14
  242.7 9.7 %collective-permute-start.13 = (bf16[16,1,128]{2,1,0:T(2,128)(2,1)S(1)}, bf16[16,1,128]{2,1,0:T(2,128)(2,1)S(1)}, u32[]{:S(2)}, u32[]{:S(2)}) collective-permute-start(bf16[16,1,128]{2,1,0:T(2,128)(2,1)S(1)} %get-tuple-element.42), channel_id=1, source_target_pairs={{1,0},{2,1},{3,2},{4,3},{5,4},{6,5},{7,6},{8,7},{9,8},{10,9},{11,1... | collective-permute-start | bytes 12296 | tf_op jit(solution)/shard_map/ppermute | solution.py:17
  248.7 9.4 %collective-permute-start.8 = (bf16[16,1,128]{2,1,0:T(2,128)(2,1)S(1)}, bf16[16,1,128]{2,1,0:T(2,128)(2,1)S(1)}, u32[]{:S(2)}, u32[]{:S(2)}) collective-permute-start(bf16[16,1,128]{2,1,0:T(2,128)(2,1)S(1)} %get-tuple-element.45), channel_id=1, source_target_pairs={{0,1},{1,2},{2,3},{3,4},{4,5},{5,6},{6,7},{7,8},{8,9},{9,10},{10,1... | collective-permute-start | bytes 12296 | tf_op jit(solution)/shard_map/ppermute | solution.py:14
  249.7 8.3 %collective-permute-start.9 = (bf16[16,1,128]{2,1,0:T(2,128)(2,1)S(1)}, bf16[16,1,128]{2,1,0:T(2,128)(2,1)S(1)}, u32[]{:S(2)}, u32[]{:S(2)}) collective-permute-start(bf16[16,1,128]{2,1,0:T(2,128)(2,1)S(1)} %get-tuple-element.46), channel_id=1, source_target_pairs={{1,0},{2,1},{3,2},{4,3},{5,4},{6,5},{7,6},{8,7},{9,8},{10,9},{11,1... | collective-permute-start | bytes 12296 | tf_op jit(solution)/shard_map/ppermute | solution.py:17
  252.4 13.2 %collective-permute-start.14 = (bf16[1,194,128]{2,1,0:T(8,128)(2,1)S(1)}, bf16[1,194,128]{2,1,0:T(8,128)(2,1)S(1)}, u32[]{:S(2)}, u32[]{:S(2)}) collective-permute-start(bf16[1,194,128]{2,1,0:T(8,128)(2,1)S(1)} %get-tuple-element.28), channel_id=1, source_target_pairs={{0,16},{16,32},{32,48},{48,64},{64,80},{80,96},{96,112},{1,17},{17... | collective-permute-start | bytes 149000 | tf_op jit(solution)/shard_map/ppermute | solution.py:14
  256.7 8.9 %collective-permute-start.15 = (bf16[1,194,128]{2,1,0:T(8,128)(2,1)S(1)}, bf16[1,194,128]{2,1,0:T(8,128)(2,1)S(1)}, u32[]{:S(2)}, u32[]{:S(2)}) collective-permute-start(bf16[1,194,128]{2,1,0:T(8,128)(2,1)S(1)} %get-tuple-element.27), channel_id=1, source_target_pairs={{16,0},{32,16},{48,32},{64,48},{80,64},{96,80},{112,96},{17,1},{33... | collective-permute-start | bytes 149000 | tf_op jit(solution)/shard_map/ppermute | solution.py:17
  258.1 17.3 %collective-permute-start.10 = (bf16[1,194,128]{2,1,0:T(8,128)(2,1)S(1)}, bf16[1,194,128]{2,1,0:T(8,128)(2,1)S(1)}, u32[]{:S(2)}, u32[]{:S(2)}) collective-permute-start(bf16[1,194,128]{2,1,0:T(8,128)(2,1)S(1)} %get-tuple-element.31), channel_id=1, source_target_pairs={{16,0},{32,16},{48,32},{64,48},{80,64},{96,80},{112,96},{17,1},{33... | collective-permute-start | bytes 149000 | tf_op jit(solution)/shard_map/ppermute | solution.py:17
  259.4 16.0 %collective-permute-start.11 = (bf16[1,194,128]{2,1,0:T(8,128)(2,1)S(1)}, bf16[1,194,128]{2,1,0:T(8,128)(2,1)S(1)}, u32[]{:S(2)}, u32[]{:S(2)}) collective-permute-start(bf16[1,194,128]{2,1,0:T(8,128)(2,1)S(1)} %get-tuple-element.32), channel_id=1, source_target_pairs={{0,16},{16,32},{32,48},{48,64},{64,80},{80,96},{96,112},{1,17},{17... | collective-permute-start | bytes 149000 | tf_op jit(solution)/shard_map/ppermute | solution.py:14
  280.8 2.1 copy-start.14
  282.9 1.1 copy-start.18
  282.9 1.6 copy-start.19
  (8 other events, 8.8 us)
Sparse Core Ops, SparseCore 0:
  280.9 150.0 all-reduce.4
